TPU v7x, 32 devices: a whole 2x2x4 slice. The times are simulated.
32 devices in a mesh: groups: 2 (over y), blk: 8 (over z, x), mp: 2 (over core).
Axes of the slice: x: 2, y: 2, z: 4, core: 2. Of those that a mesh axis runs over, the one named last changes fastest.
Arguments:
- probe_vectors: bfloat16 [12, 8, 32, 3584], P('groups', 'blk', None, 'mp'), parts along dimension 0, may hold values from -12 to 12
- unsettled_lookups: bfloat16 [12, 8, 32, 512], P('groups', 'blk', None, 'mp'), parts along dimension 0, may hold values from -6 to 6
- unsettled_payloads: bfloat16 [12, 8, 32, 512], P('groups', 'blk', None, 'mp'), parts along dimension 0, may hold values from -6 to 6
- uncover_ordering: int32 [12, 8, 32], P('groups', 'blk'), parts along dimension 0, may hold values from 0 to 31, each once within a row
- rounds_finished: int32 [12, 8], P('groups', 'blk'), parts along dimension 0, may hold values from 0 to 7
- random_entry_choice: int32 [12, 8, 32], P('groups', 'blk'), parts along dimension 0, may hold values from 0 to 63
- noise_token_keys: bfloat16 [64, 512], P(None, 'mp'), may hold values from -6 to 6
- noise_token_values: bfloat16 [64, 512], P(None, 'mp'), may hold values from -6 to 6
- prefix_key_cache: bfloat16 [2, 8, 32, 512], P('groups', 'blk', None, 'mp'), parts along dimension 0, may hold values from -6 to 6
- prefix_value_cache: bfloat16 [2, 8, 32, 512], P('groups', 'blk', None, 'mp'), parts along dimension 0, may hold values from -6 to 6
- completed_keys: bfloat16 [16, 32, 512], P(('groups', 'blk'), None, 'mp'), parts along dimension 0, may hold values from -6 to 6
- completed_values: bfloat16 [16, 32, 512], P(('groups', 'blk'), None, 'mp'), parts along dimension 0, may hold values from -6 to 6
- committing_index: int32 [2], P('groups'), parts along dimension 0, may hold values from 0 to 7, as said below
Outputs:
- attended: bfloat16 [12, 8, 32, 3584], P('groups', 'blk', None, 'mp'), parts along dimension 0
There are 2 independent parts, one for each index of `groups`. A program takes and returns all parts, laid end to end along the dimension named above; an argument that names none is the same for every part. Nothing has to cross between parts.
Inputs may be any that keep to these rules, and one draw needn't show every extreme that they name: `committing_index`: an index of blk; in every odd part it is the last index, 7.
All inputs are finite; a program needn't handle non-finite values.
Results may differ from a plain program's by a relative error of at most 0.005.
Values may be sent and summed in bfloat16 or wider, within the bound.
No kernel may reach another device: no remote copies, remote signals or barrier semaphores. Data moves between devices by JAX's collectives and lax.ppermute only.
A program may use at most 128 MiB of HBM per device.

v0:
```python
import math

import jax
import jax.numpy as jnp
from jax import lax
from jax.experimental import pallas as pl
from jax.experimental.pallas import tpu as pltpu
from jax.sharding import PartitionSpec as P


QUERY_GROUPS = 28
MEMORY_GROUPS = 4
FEATURE_DIM = 128
UNMASK = 4
GROUP = QUERY_GROUPS // MEMORY_GROUPS
RATE = FEATURE_DIM ** (-0.5) * math.log2(math.e)

SMALL = 8


def column(row):
    n = row.shape[1]
    here = lax.broadcasted_iota(jnp.int32, (n, n), 0)
    there = lax.broadcasted_iota(jnp.int32, (n, n), 1)
    return jnp.sum(jnp.where(here == there, row, 0), axis=1, keepdims=True)


def blend_kernel(
    rounds, order_at, choice_at, table_k_at, table_v_at, open_k_at, open_v_at, own, *scratch
):
    sources = (order_at, choice_at, table_k_at, table_v_at, open_k_at, open_v_at)
    order, choice, table_k, table_v, open_k, open_v, sems = scratch
    copies = [
        pltpu.make_async_copy(src, dst, sems.at[i])
        for i, (src, dst) in enumerate(zip(sources, scratch))
    ]
    for copy in copies:
        copy.start()
    for copy in copies:
        copy.wait()
    slots, block = open_k.shape[0], open_k.shape[2]
    nrows = table_k.shape[0]
    masks, hots = [], []
    for s in range(slots):
        masks.append(column(jnp.where(order[s] >= UNMASK * rounds[s], 1, 0)) > 0)
        picked = column(choice[s])
        hots.append(
            jnp.where(picked == lax.broadcasted_iota(jnp.int32, (block, nrows), 1), 1.0, 0.0)
        )
    onehot = jnp.concatenate(hots, axis=0).astype(jnp.bfloat16)
    for i, (table, opened) in enumerate(((table_k, open_k), (table_v, open_v))):
        noise = jnp.dot(onehot, table[...], preferred_element_type=jnp.float32)
        for s in range(slots):
            mixed = jnp.where(
                masks[s], noise[s * block : (s + 1) * block], opened[s, 0].astype(jnp.float32)
            )
            own[s, i] = mixed.astype(jnp.bfloat16)


def scores(query, slot, head, keys):
    q = jnp.concatenate(
        [
            query[slot, :, (head * GROUP + g) * FEATURE_DIM : (head * GROUP + g + 1) * FEATURE_DIM]
            for g in range(GROUP)
        ],
        axis=0,
    )
    return lax.dot_general(
        q, keys, (((1,), (1,)), ((), ())), preferred_element_type=jnp.float32
    )


def spread(top, n):
    times = -(-n // top.shape[1])
    return jnp.concatenate([top] * times, axis=1)[:, :n]


def each_slot(slots, blocks, body):
    if blocks <= SMALL:
        for s in range(slots):
            body(s)
    else:
        pl.loop(0, slots)(body)


def grant(blocks):
    return pltpu.CompilerParams(vmem_limit_bytes=20 << 20) if blocks <= SMALL else None


def first_kernel(query, near, own, tops, totals, sums):
    slots, _, _, width = own.shape
    last = near.shape[0] - 1

    def attend(s):
        for h in range(width // FEATURE_DIM):
            cols = slice(h * FEATURE_DIM, (h + 1) * FEATURE_DIM)

            def stack(i):
                parts = [near[b, i, :, cols] for b in range(last)] + [own[s, i, :, cols]]
                return jnp.concatenate(parts, axis=0)

            score = scores(query, s, h, stack(0))
            top = jnp.max(score, axis=1, keepdims=True)
            weight = jnp.exp2((score - top) * RATE)
            tops[s, h] = jnp.broadcast_to(top, tops.shape[2:])
            totals[s, h] = jnp.broadcast_to(
                jnp.sum(weight, axis=1, keepdims=True), totals.shape[2:]
            )
            sums[s, h] = jnp.dot(
                weight.astype(jnp.bfloat16), stack(1), preferred_element_type=jnp.float32
            )

    each_slot(slots, last, attend)


def last_kernel(rounds, order, info, query, near, far, prev, tops, totals, sums, out, made, sems):
    slots, _, block, width = prev.shape
    last = near.shape[0] - 1
    take = info[1] > 0

    def copy_of(s):
        return pltpu.make_async_copy(made.at[s], out.at[s], sems.at[s])

    def attend(s):
        came = lax.rem(s + slots - info[0], slots)
        mask = column(jnp.where(order[s] >= UNMASK * rounds[s], 1, 0)) > 0
        for h in range(width // FEATURE_DIM):
            cols = slice(h * FEATURE_DIM, (h + 1) * FEATURE_DIM)

            def stack(i):
                parts = [far[b, i, :, cols] for b in range(last)]
                parts.append(jnp.where(take, near[last, i, :, cols], far[last, i, :, cols]))
                parts.append(prev[came, i, :, cols])
                return jnp.concatenate(parts, axis=0)

            score = scores(query, s, h, stack(0))
            before = tops[s, h]
            top = jnp.maximum(before, jnp.max(score, axis=1, keepdims=True))
            factor = jnp.exp2((before - top) * RATE)
            weight = jnp.exp2((score - spread(top, score.shape[1])) * RATE)
            total = totals[s, h] * factor + jnp.sum(weight, axis=1, keepdims=True)
            context = sums[s, h] * factor + jnp.dot(
                weight.astype(jnp.bfloat16), stack(1), preferred_element_type=jnp.float32
            )
            context = context / total
            for g in range(GROUP):
                part = jnp.where(mask, context[g * block : (g + 1) * block], 0.0)
                at = (h * GROUP + g) * FEATURE_DIM
                made[s, :, at : at + FEATURE_DIM] = part.astype(jnp.bfloat16)
        copy_of(s).start()

    each_slot(slots, last, attend)
    each_slot(slots, last, lambda s: copy_of(s).wait())


def swap(block, axis, bit):
    size = lax.axis_size(axis)
    return lax.ppermute(block, axis, [(i, i ^ bit) for i in range(size)])


def on_device(
    probe_vectors,
    unsettled_lookups,
    unsettled_payloads,
    uncover_ordering,
    rounds_finished,
    random_entry_choice,
    noise_token_keys,
    noise_token_values,
    prefix_key_cache,
    prefix_value_cache,
    completed_keys,
    completed_values,
    committing_index,
):
    slots, block = probe_vectors.shape[0], probe_vectors.shape[2]
    wide = probe_vectors.shape[3]
    width = noise_token_keys.shape[1]
    size = lax.axis_size("blk")
    me = lax.axis_index("blk")
    owner = committing_index[0]
    rounds = rounds_finished.reshape(slots)

    vm = pl.BlockSpec(memory_space=pltpu.VMEM)
    sm = pl.BlockSpec(memory_space=pltpu.SMEM)

    packed = jnp.stack(
        [
            a.reshape(block, width)
            for a in (prefix_key_cache, prefix_value_cache, completed_keys, completed_values)
        ]
    ).reshape(2, 2, block, width)
    sources = (
        uncover_ordering,
        random_entry_choice,
        noise_token_keys,
        noise_token_values,
        unsettled_lookups,
        unsettled_payloads,
    )
    blend = pl.pallas_call(
        blend_kernel,
        out_shape=jax.ShapeDtypeStruct((slots, 2, block, width), jnp.bfloat16),
        in_specs=[sm] + [pl.BlockSpec(memory_space=pltpu.HBM)] * len(sources),
        out_specs=vm,
        scratch_shapes=[pltpu.VMEM(a.shape, a.dtype) for a in sources]
        + [pltpu.SemaphoreType.DMA((len(sources),))],
        name="blend",
    )
    own = blend(rounds, *sources)
    prev = lax.ppermute(own, "blk", [(i, (i + 1) % size) for i in range(size)])
    bit = size // 2
    while True:
        packed = lax.optimization_barrier(packed)
        got = swap(packed, "blk", bit)
        same = (owner & bit) == (me & bit)
        if bit == 1:
            break
        pick = jnp.where(same, packed[-1:], got[-1:])
        packed = jnp.concatenate([packed[:-1], got[:-1], pick], axis=0)
        bit //= 2

    info = jnp.stack([(me == 0).astype(jnp.int32), same.astype(jnp.int32)])
    heads = width // FEATURE_DIM
    query = probe_vectors.reshape(slots, block, wide)
    part = jax.ShapeDtypeStruct((slots, heads, GROUP * block, FEATURE_DIM), jnp.float32)
    state = pl.pallas_call(
        first_kernel,
        out_shape=[part] * 3,
        in_specs=[vm] * 3,
        out_specs=[vm] * 3,
        compiler_params=grant(size // 2),
        name="early",
    )(query, packed, own)
    out = pl.pallas_call(
        last_kernel,
        out_shape=jax.ShapeDtypeStruct((slots, block, wide), jnp.bfloat16),
        in_specs=[sm, vm, sm] + [vm] * 7,
        out_specs=pl.BlockSpec(memory_space=pl.ANY),
        scratch_shapes=[
            pltpu.VMEM((slots, block, wide), jnp.bfloat16),
            pltpu.SemaphoreType.DMA((slots,)),
        ],
        compiler_params=grant(size // 2),
        name="late",
    )(rounds, uncover_ordering, info, query, packed, got, prev, *state)
    return out.reshape(slots, 1, block, wide)


def solution(mesh):
    placed = (
        P("groups", "blk", None, "mp"),
        P("groups", "blk", None, "mp"),
        P("groups", "blk", None, "mp"),
        P("groups", "blk", None),
        P("groups", "blk"),
        P("groups", "blk", None),
        P(None, "mp"),
        P(None, "mp"),
        P("groups", "blk", None, "mp"),
        P("groups", "blk", None, "mp"),
        P(("groups", "blk"), None, "mp"),
        P(("groups", "blk"), None, "mp"),
        P("groups"),
    )

    return jax.shard_map(
        on_device,
        mesh=mesh,
        in_specs=placed,
        out_specs=P("groups", "blk", None, "mp"),
        check_vma=False,
    )
```

profile of v0, /device:TPU:0, one launch (start us, length us, event | category | flops | bytes accessed | tf_op | source)
XLA Modules:
  0.0 25.9 jit_solution(18205910373785586195)
XLA Ops:
  0.0 0.0 copy-start
  0.0 0.8 %pad_maximum_fusion.2 = bf16[4,32,256]{2,1,0:T(8,128)(2,1)S(1)} fusion(bf16[1,32,256]{2,1,0:T(8,128)(2,1)} %param.24, bf16[1,32,256]{2,1,0:T(8,128)(2,1)} %param.23, bf16[1,32,256]{2,1,0:T(8,128)(2,1)} %bitcast.19, bf16[1,32,256]{2,1,0:T(8,128)(2,1)} %bitcast.20), kind=kLoop, calls=%fused_computation.2 | loop fusion | flops 98304 | bytes 131072 | tf_op jit(solution)/shard_map/stack | solution.py:187
  0.8 0.0 copy-start.2
  0.9 0.0 copy-start.3
  0.9 4.1 %collective-permute-start = (bf16[2,2,32,256]{3,2,1,0:T(8,128)(2,1)S(1)}, bf16[2,2,32,256]{3,2,1,0:T(8,128)(2,1)S(1)}, u32[]{:S(2)}, u32[]{:S(2)}) collective-permute-start(bf16[2,2,32,256]{3,2,1,0:T(8,128)(2,1)S(1)} %bitcast.17), channel_id=1, source_target_pairs={{0,8},{2,10},{4,12},{6,14},{8,0},{10,2},{12,4},{14,6},{1,9},{3,11}... | collective-permute-start | bytes 196616 | tf_op jit(solution)/shard_map/ppermute | solution.py:158
  5.7 3.0 %collective-permute-done = bf16[2,2,32,256]{3,2,1,0:T(8,128)(2,1)S(1)} collective-permute-done((bf16[2,2,32,256]{3,2,1,0:T(8,128)(2,1)S(1)}, bf16[2,2,32,256]{3,2,1,0:T(8,128)(2,1)S(1)}, u32[]{:S(2)}, u32[]{:S(2)}) %collective-permute-start) | collective-permute-done | bytes 65568 | tf_op jit(solution)/shard_map/ppermute | solution.py:158
  8.7 0.6 %collective-permute-start.1 = (bf16[3,2,32,256]{3,2,1,0:T(8,128)(2,1)S(1)}, bf16[3,2,32,256]{3,2,1,0:T(8,128)(2,1)S(1)}, u32[]{:S(2)}, u32[]{:S(2)}) collective-permute-start(bf16[3,2,32,256]{3,2,1,0:T(8,128)(2,1)S(1)} %pad_maximum_fusion.1), channel_id=1, source_target_pairs={{0,4},{2,6},{4,0},{6,2},{8,12},{10,14},{12,8},{14,10},{1,5},{3,7},... | collective-permute-start | bytes 294920 | tf_op jit(solution)/shard_map/ppermute | solution.py:158
  9.3 2.7 %blend.1.own = bf16[6,2,32,256]{3,2,1,0:T(8,128)(2,1)} custom-call(s32[6]{0:T(128)} %bitcast.15, s32[6,1,32]{2,1,0:T(1,128)} %order.1, s32[6,1,32]{2,1,0:T(1,128)} %choice_at.1, bf16[64,256]{1,0:T(8,128)(2,1)} %table_k_at.1, bf16[64,256]{1,0:T(8,128)(2,1)} %table_v_at.1, bf16[6,1,32,256]{3,2,1,0:T(8,128)(2,1)} %open_k_at.1, bf16[6,1,32,256]{3,2,1,0:T(8,128)(2,1)} %open_v_at.1), custom_call_target="tpu_custom_call" | custom-call | tf_op jit(solution)/shard_map/blend/pallas_call | solution.py:210
  12.0 1.5 %collective-permute-start.3 = (bf16[6,2,32,256]{3,2,1,0:T(8,128)(2,1)}, bf16[6,2,32,256]{3,2,1,0:T(8,128)(2,1)S(1)}, u32[]{:S(2)}, u32[]{:S(2)}) collective-permute-start(bf16[6,2,32,256]{3,2,1,0:T(8,128)(2,1)} %blend.1.own), channel_id=1, source_target_pairs={{0,2},{2,4},{4,6},{6,8},{8,10},{10,12},{12,14},{14,0},{1,3},{3,5},... | collective-permute-start | bytes 589832 | tf_op jit(solution)/shard_map/ppermute | solution.py:211
  13.6 0.0 collective-permute-done.1
  13.6 1.6 %collective-permute-start.2 = (bf16[5,2,32,256]{3,2,1,0:T(8,128)(2,1)S(1)}, bf16[5,2,32,256]{3,2,1,0:T(8,128)(2,1)S(1)}, u32[]{:S(2)}, u32[]{:S(2)}) collective-permute-start(bf16[5,2,32,256]{3,2,1,0:T(8,128)(2,1)S(1)} %pad_maximum_fusion.near), channel_id=1, source_target_pairs={{0,2},{2,0},{4,6},{6,4},{8,10},{10,8},{12,14},{14,12},{1,3},{3,1},... | collective-permute-start | bytes 491528 | tf_op jit(solution)/shard_map/ppermute | solution.py:158
  15.2 0.1 add_convert_fusion.info
  15.3 0.0 copy-done
  15.3 0.0 copy-start.1
  15.3 0.9 %copy-done.1 = bf16[6,2,32,256]{3,2,1,0:T(8,128)(2,1)S(1)} copy-done((bf16[6,2,32,256]{3,2,1,0:T(8,128)(2,1)S(1)}, bf16[6,2,32,256]{3,2,1,0:T(8,128)(2,1)}, u32[]{:S(2)}) %copy-start.1) | copy-done | bytes 196632
  16.2 1.3 %early.1 = (f32[6,2,224,128]{3,2,1,0:T(8,128)S(1)}, f32[6,2,224,128]{3,2,1,0:T(8,128)S(1)}, f32[6,2,224,128]{3,2,1,0:T(8,128)S(1)}) custom-call(bf16[6,32,1792]{2,1,0:T(8,128)(2,1)S(1)} %bitcast.13, bf16[5,2,32,256]{3,2,1,0:T(8,128)(2,1)S(1)} %pad_maximum_fusion.near, bf16[6,2,32,256]{3,2,1,0:T(8,128)(2,1)S(1)} %copy-done.1), custom_call_target="tpu_custom_call" | custom-call | tf_op jit(solution)/shard_map/early/pallas_call | solution.py:227
  17.5 3.7 %collective-permute-done.3.prev = bf16[6,2,32,256]{3,2,1,0:T(8,128)(2,1)S(1)} collective-permute-done((bf16[6,2,32,256]{3,2,1,0:T(8,128)(2,1)}, bf16[6,2,32,256]{3,2,1,0:T(8,128)(2,1)S(1)}, u32[]{:S(2)}, u32[]{:S(2)}) %collective-permute-start.3) | collective-permute-done | bytes 196640 | tf_op jit(solution)/shard_map/ppermute | solution.py:211
  21.1 1.9 %collective-permute-done.2.far = bf16[5,2,32,256]{3,2,1,0:T(8,128)(2,1)S(1)} collective-permute-done((bf16[5,2,32,256]{3,2,1,0:T(8,128)(2,1)S(1)}, bf16[5,2,32,256]{3,2,1,0:T(8,128)(2,1)S(1)}, u32[]{:S(2)}, u32[]{:S(2)}) %collective-permute-start.2) | collective-permute-done | bytes 163872 | tf_op jit(solution)/shard_map/ppermute | solution.py:158
  23.0 0.0 copy-done.2
  23.0 0.0 copy-done.3
  23.0 2.9 %late.1 = bf16[6,32,1792]{2,1,0:T(8,128)(2,1)} custom-call(s32[6]{0:T(128)S(1)} %bitcast.16, s32[6,1,32]{2,1,0:T(1,128)S(1)} %copy-done.2, s32[2]{0:T(128)S(1)} %add_convert_fusion.info, bf16[6,32,1792]{2,1,0:T(8,128)(2,1)S(1)} %bitcast.14, bf16[5,2,32,256]{3,2,1,0:T(8,128)(2,1)S(1)} %pad_maximum_fusion.near, ...), custom_call_target="tpu_custom_call" | custom-call | tf_op jit(solution)/shard_map/late/pallas_call | solution.py:235
  (6 shorter events, 0.1 us)
Async XLA Ops:
  0.0 15.3 %copy-start = (bf16[6,1,32,1792]{3,2,1,0:T(8,128)(2,1)S(1)}, bf16[6,1,32,1792]{3,2,1,0:T(8,128)(2,1)}, u32[]{:S(2)}) copy-start(bf16[6,1,32,1792]{3,2,1,0:T(8,128)(2,1)} %param.13) | copy-start | bytes 2064388
  0.8 22.1 %copy-start.2 = (s32[6,1,32]{2,1,0:T(1,128)S(1)}, s32[6,1,32]{2,1,0:T(1,128)}, u32[]{:S(2)}) copy-start(s32[6,1,32]{2,1,0:T(1,128)} %order.1) | copy-start | bytes 2308
  0.9 22.1 %copy-start.3 = (s32[6,1]{0,1:T(1,128)S(1)}, s32[6,1]{0,1:T(1,128)}, u32[]{:S(2)}) copy-start(s32[6,1]{0,1:T(1,128)} %param.17) | copy-start | bytes 76
  0.9 7.8 %collective-permute-start = (bf16[2,2,32,256]{3,2,1,0:T(8,128)(2,1)S(1)}, bf16[2,2,32,256]{3,2,1,0:T(8,128)(2,1)S(1)}, u32[]{:S(2)}, u32[]{:S(2)}) collective-permute-start(bf16[2,2,32,256]{3,2,1,0:T(8,128)(2,1)S(1)} %bitcast.17), channel_id=1, source_target_pairs={{0,8},{2,10},{4,12},{6,14},{8,0},{10,2},{12,4},{14,6},{1,9},{3,11}... | collective-permute-start | bytes 196616 | tf_op jit(solution)/shard_map/ppermute | solution.py:158
  8.7 4.9 %collective-permute-start.1 = (bf16[3,2,32,256]{3,2,1,0:T(8,128)(2,1)S(1)}, bf16[3,2,32,256]{3,2,1,0:T(8,128)(2,1)S(1)}, u32[]{:S(2)}, u32[]{:S(2)}) collective-permute-start(bf16[3,2,32,256]{3,2,1,0:T(8,128)(2,1)S(1)} %pad_maximum_fusion.1), channel_id=1, source_target_pairs={{0,4},{2,6},{4,0},{6,2},{8,12},{10,14},{12,8},{14,10},{1,5},{3,7},... | collective-permute-start | bytes 294920 | tf_op jit(solution)/shard_map/ppermute | solution.py:158
  12.0 9.1 %collective-permute-start.3 = (bf16[6,2,32,256]{3,2,1,0:T(8,128)(2,1)}, bf16[6,2,32,256]{3,2,1,0:T(8,128)(2,1)S(1)}, u32[]{:S(2)}, u32[]{:S(2)}) collective-permute-start(bf16[6,2,32,256]{3,2,1,0:T(8,128)(2,1)} %blend.1.own), channel_id=1, source_target_pairs={{0,2},{2,4},{4,6},{6,8},{8,10},{10,12},{12,14},{14,0},{1,3},{3,5},... | collective-permute-start | bytes 589832 | tf_op jit(solution)/shard_map/ppermute | solution.py:211
  13.6 9.4 %collective-permute-start.2 = (bf16[5,2,32,256]{3,2,1,0:T(8,128)(2,1)S(1)}, bf16[5,2,32,256]{3,2,1,0:T(8,128)(2,1)S(1)}, u32[]{:S(2)}, u32[]{:S(2)}) collective-permute-start(bf16[5,2,32,256]{3,2,1,0:T(8,128)(2,1)S(1)} %pad_maximum_fusion.near), channel_id=1, source_target_pairs={{0,2},{2,0},{4,6},{6,4},{8,10},{10,8},{12,14},{14,12},{1,3},{3,1},... | collective-permute-start | bytes 491528 | tf_op jit(solution)/shard_map/ppermute | solution.py:158
  15.3 0.9 %copy-start.1 = (bf16[6,2,32,256]{3,2,1,0:T(8,128)(2,1)S(1)}, bf16[6,2,32,256]{3,2,1,0:T(8,128)(2,1)}, u32[]{:S(2)}) copy-start(bf16[6,2,32,256]{3,2,1,0:T(8,128)(2,1)} %blend.1.own) | copy-start | bytes 589828
where the time goes:
time: 26.1 us; the launch traced here: 25.9 us
  waiting for transfers between devices  8.51 us (33%)
  starting transfers between devices  7.87 us (30%)
  Pallas kernels  6.83 us (26%)
  other arithmetic  0.98 us (4%)
  local copies, waits for them, and re-layouts  0.95 us (4%)
  between operations  0.74 us (3%)
    ppermute x3, starting transfers between devices, swap(): return lax.ppermute(block, axis, [(i, i ^ bit) for i in range(size)])  6.32 us
    ppermute x3, waiting for transfers between devices, swap(): return lax.ppermute(block, axis, [(i, i ^ bit) for i in range(size)])  4.85 us
    ppermute x1, waiting for transfers between devices, on_device(): prev = lax.ppermute(own, 'blk', [(i, (i + 1) % size) for i in range(size)])  3.66 us
    pallas_call x1, Pallas kernels, on_device(): pl.pallas_call(last_kernel, out_shape=jax.ShapeDtypeStruct((slots, block,...  2.88 us
    pallas_call x1, Pallas kernels, on_device(): own = blend(rounds, *sources)  2.67 us
    ppermute x1, starting transfers between devices, on_device(): prev = lax.ppermute(own, 'blk', [(i, (i + 1) % size) for i in range(size)])  1.54 us
    pallas_call x1, Pallas kernels, on_device(): pl.pallas_call(first_kernel, out_shape=[part] * 3, in_specs=[vm] * 3, out...  1.28 us
    unnamed x8, local copies, waits for them, and re-layouts  0.94 us
  transfers between devices with their start and end apart: 4, of which 3 were waited for; matrix products, arithmetic and copies ran while one was open for 0% of the time, Pallas kernels for 15%

commit v1 on v0

v1 whole, which is shorter than its diff:
```python
import math

import jax
import jax.numpy as jnp
from jax import lax
from jax.experimental import pallas as pl
from jax.experimental.pallas import tpu as pltpu
from jax.sharding import PartitionSpec as P


QUERY_GROUPS = 28
MEMORY_GROUPS = 4
FEATURE_DIM = 128
UNMASK = 4
GROUP = QUERY_GROUPS // MEMORY_GROUPS
RATE = FEATURE_DIM ** (-0.5) * math.log2(math.e)

SMALL = 8


def column(row):
    n = row.shape[1]
    here = lax.broadcasted_iota(jnp.int32, (n, n), 0)
    there = lax.broadcasted_iota(jnp.int32, (n, n), 1)
    return jnp.sum(jnp.where(here == there, row, 0), axis=1, keepdims=True)


def blend_kernel(
    rounds, turn, order_at, choice_at, table_k_at, table_v_at, open_k_at, open_v_at, own, *scratch
):
    sources = (order_at, choice_at, table_k_at, table_v_at, open_k_at, open_v_at)
    order, choice, table_k, table_v, open_k, open_v, sems = scratch
    copies = [
        pltpu.make_async_copy(src, dst, sems.at[i])
        for i, (src, dst) in enumerate(zip(sources, scratch))
    ]
    for copy in copies:
        copy.start()
    for copy in copies:
        copy.wait()
    slots, block = open_k.shape[0], open_k.shape[2]
    nrows = table_k.shape[0]
    masks, hots = [], []
    for s in range(slots):
        masks.append(column(jnp.where(order[s] >= UNMASK * rounds[s], 1, 0)) > 0)
        picked = column(choice[s])
        hots.append(
            jnp.where(picked == lax.broadcasted_iota(jnp.int32, (block, nrows), 1), 1.0, 0.0)
        )
    onehot = jnp.concatenate(hots, axis=0).astype(jnp.bfloat16)
    for i, (table, opened) in enumerate(((table_k, open_k), (table_v, open_v))):
        noise = jnp.dot(onehot, table[...], preferred_element_type=jnp.float32)
        for s in range(slots):
            mixed = jnp.where(
                masks[s], noise[s * block : (s + 1) * block], opened[s, 0].astype(jnp.float32)
            )
            own[lax.rem(s + turn[0], slots), i] = mixed.astype(jnp.bfloat16)


def scores(query, slot, head, keys):
    q = jnp.concatenate(
        [
            query[slot, :, (head * GROUP + g) * FEATURE_DIM : (head * GROUP + g + 1) * FEATURE_DIM]
            for g in range(GROUP)
        ],
        axis=0,
    )
    return lax.dot_general(
        keys, q, (((1,), (1,)), ((), ())), preferred_element_type=jnp.float32
    )


def gathered(values, weight):
    return lax.dot_general(
        values,
        weight,
        (((0,), (0,)), ((), ())),
        preferred_element_type=jnp.float32,
    )


def staggered(slots, heads, blocks, stages):
    def run(tasks):
        held = {}
        for step in range(len(tasks) + len(stages) - 1):
            for k, stage in enumerate(stages):
                i = step - k
                if 0 <= i < len(tasks):
                    held[i] = stage(*tasks[i], *held.get(i, ()))

    if blocks <= SMALL:
        run([(s, h) for s in range(slots) for h in range(heads)])
    else:
        pl.loop(0, slots)(lambda s: run([(s, h) for h in range(heads)]))


def grant(blocks):
    return pltpu.CompilerParams(vmem_limit_bytes=20 << 20) if blocks <= SMALL else None


def columns(head):
    return slice(head * FEATURE_DIM, (head + 1) * FEATURE_DIM)


def first_kernel(rounds, turn, took, order, query, near, own, tops, totals, sums, keep, mine):
    slots, _, _, width = own.shape
    last = near.shape[0] - 1
    mine[...] = jnp.full(mine.shape, took[0], jnp.int32)

    def stack(s, h, i):
        at = lax.rem(s + turn[0], slots)
        parts = [near[b, i, :, columns(h)] for b in range(last)] + [own[at, i, :, columns(h)]]
        return jnp.concatenate(parts, axis=0)

    def score(s, h):
        if h == 0:
            masked = jnp.where(order[s] >= UNMASK * rounds[s], 1.0, 0.0)
            keep[s] = jnp.concatenate([masked] * GROUP, axis=1)
        return (scores(query, s, h, stack(s, h, 0)),)

    def peak(s, h, score):
        top = jnp.max(score, axis=0, keepdims=True)
        tops[s, h] = top
        return score, top

    def weigh(s, h, score, top):
        weight = jnp.exp2((score - top) * RATE)
        totals[s, h] = jnp.sum(weight, axis=0, keepdims=True)
        return (weight.astype(jnp.bfloat16),)

    def gather(s, h, weight):
        sums[s, h] = gathered(stack(s, h, 1), weight)

    staggered(slots, width // FEATURE_DIM, last, (score, peak, weigh, gather))


def last_kernel(query, near, far, prev, tops, totals, sums, keep, mine, out, made, sems):
    slots, _, block, width = prev.shape
    heads = width // FEATURE_DIM
    last = near.shape[0] - 1
    take = mine[:1, :] > 0

    def copy_of(s):
        return pltpu.make_async_copy(made.at[s], out.at[s], sems.at[s])

    def stack(s, h, i):
        parts = [far[b, i, :, columns(h)] for b in range(last)]
        parts.append(jnp.where(take, near[last, i, :, columns(h)], far[last, i, :, columns(h)]))
        parts.append(prev[s, i, :, columns(h)])
        return jnp.concatenate(parts, axis=0)

    def score(s, h):
        return (scores(query, s, h, stack(s, h, 0)),)

    def peak(s, h, score):
        before = tops[s, h]
        top = jnp.maximum(before, jnp.max(score, axis=0, keepdims=True))
        return score, top, jnp.exp2((before - top) * RATE)

    def weigh(s, h, score, top, factor):
        weight = jnp.exp2((score - top) * RATE)
        total = totals[s, h] * factor + jnp.sum(weight, axis=0, keepdims=True)
        share = jnp.where(keep[s] > 0, 1.0 / total, 0.0)
        return weight.astype(jnp.bfloat16), factor * share, share

    def gather(s, h, weight, old, share):
        return gathered(stack(s, h, 1), weight), old, share

    def finish(s, h, context, old, share):
        context = sums[s, h] * old + context * share
        context = jnp.transpose(context.astype(jnp.bfloat16))
        for g in range(GROUP):
            at = (h * GROUP + g) * FEATURE_DIM
            made[s, :, at : at + FEATURE_DIM] = context[g * block : (g + 1) * block]
        if h == heads - 1:
            copy_of(s).start()

    staggered(slots, heads, last, (score, peak, weigh, gather, finish))
    staggered(slots, 1, last, (lambda s, h: copy_of(s).wait(),))


def swap(block, axis, bit):
    size = lax.axis_size(axis)
    return lax.ppermute(block, axis, [(i, i ^ bit) for i in range(size)])


def on_device(
    probe_vectors,
    unsettled_lookups,
    unsettled_payloads,
    uncover_ordering,
    rounds_finished,
    random_entry_choice,
    noise_token_keys,
    noise_token_values,
    prefix_key_cache,
    prefix_value_cache,
    completed_keys,
    completed_values,
    committing_index,
):
    slots, block = probe_vectors.shape[0], probe_vectors.shape[2]
    wide = probe_vectors.shape[3]
    width = noise_token_keys.shape[1]
    size = lax.axis_size("blk")
    me = lax.axis_index("blk")
    owner = committing_index[0]
    rounds = rounds_finished.reshape(slots)
    turn = (me == size - 1).astype(jnp.int32).reshape(1)

    vm = pl.BlockSpec(memory_space=pltpu.VMEM)
    sm = pl.BlockSpec(memory_space=pltpu.SMEM)

    packed = jnp.stack(
        [
            a.reshape(block, width)
            for a in (prefix_key_cache, prefix_value_cache, completed_keys, completed_values)
        ]
    ).reshape(2, 2, block, width)
    sources = (
        uncover_ordering,
        random_entry_choice,
        noise_token_keys,
        noise_token_values,
        unsettled_lookups,
        unsettled_payloads,
    )
    blend = pl.pallas_call(
        blend_kernel,
        out_shape=jax.ShapeDtypeStruct((slots, 2, block, width), jnp.bfloat16),
        in_specs=[sm] * 2 + [pl.BlockSpec(memory_space=pltpu.HBM)] * len(sources),
        out_specs=vm,
        scratch_shapes=[pltpu.VMEM(a.shape, a.dtype) for a in sources]
        + [pltpu.SemaphoreType.DMA((len(sources),))],
        name="blend",
    )
    own = blend(rounds, turn, *sources)
    prev = lax.ppermute(own, "blk", [(i, (i + 1) % size) for i in range(size)])
    bits = [1 << b for b in reversed(range(size.bit_length() - 1))]
    bits[-2:] = bits[:-3:-1]
    for hop, bit in enumerate(bits):
        packed = lax.optimization_barrier(packed)
        got = swap(packed, "blk", bit)
        same = (owner & bit) == (me & bit)
        if hop < len(bits) - 1:
            pick = jnp.where(same, packed[-1:], got[-1:])
            packed = jnp.concatenate([packed[:-1], got[:-1], pick], axis=0)

    took = same.astype(jnp.int32).reshape(1)
    heads = width // FEATURE_DIM
    query = probe_vectors.reshape(slots, block, wide)
    shapes = [(slots, heads, n, GROUP * block) for n in (1, 1, FEATURE_DIM)]
    shapes = [jax.ShapeDtypeStruct(a, jnp.float32) for a in shapes]
    shapes.append(jax.ShapeDtypeStruct((slots, 1, GROUP * block), jnp.float32))
    shapes.append(jax.ShapeDtypeStruct((8, FEATURE_DIM), jnp.int32))
    state = pl.pallas_call(
        first_kernel,
        out_shape=shapes,
        in_specs=[sm] * 3 + [vm] * 4,
        out_specs=[vm] * len(shapes),
        compiler_params=grant(size // 2),
        name="early",
    )(rounds, turn, took, uncover_ordering, query, packed, own)
    out = pl.pallas_call(
        last_kernel,
        out_shape=jax.ShapeDtypeStruct((slots, block, wide), jnp.bfloat16),
        in_specs=[vm] * (4 + len(shapes)),
        out_specs=pl.BlockSpec(memory_space=pl.ANY),
        scratch_shapes=[
            pltpu.VMEM((slots, block, wide), jnp.bfloat16),
            pltpu.SemaphoreType.DMA((slots,)),
        ],
        compiler_params=grant(size // 2),
        name="late",
    )(query, packed, got, prev, *state)
    return out.reshape(slots, 1, block, wide)


def solution(mesh):
    placed = (
        P("groups", "blk", None, "mp"),
        P("groups", "blk", None, "mp"),
        P("groups", "blk", None, "mp"),
        P("groups", "blk", None),
        P("groups", "blk"),
        P("groups", "blk", None),
        P(None, "mp"),
        P(None, "mp"),
        P("groups", "blk", None, "mp"),
        P("groups", "blk", None, "mp"),
        P(("groups", "blk"), None, "mp"),
        P(("groups", "blk"), None, "mp"),
        P("groups"),
    )

    return jax.shard_map(
        on_device,
        mesh=mesh,
        in_specs=placed,
        out_specs=P("groups", "blk", None, "mp"),
        check_vma=False,
    )
```

time: 26.1 us -> 25.5 us (0.977)
  starting transfers between devices: 7.87 us -> 6.82 us
  waiting for transfers between devices: 8.51 us -> 9.25 us
    ppermute x1, waiting for transfers between devices: 3.66 us -> 6.14 us  [on_device(): prev = lax.ppermute(own, 'blk', [(i, (i + 1) % size) for i in range(size)])]
    ppermute x3, waiting for transfers between devices: 4.85 us -> 3.11 us  [swap(): return lax.ppermute(block, axis, [(i, i ^ bit) for i in range(size)])]
    ppermute x1, starting transfers between devices: 1.54 us -> 0.38 us  [on_device(): prev = lax.ppermute(own, 'blk', [(i, (i + 1) % size) for i in range(size)])]
    pallas_call x1, Pallas kernels: 2.88 us -> 2.19 us  [on_device(): pl.pallas_call(last_kernel, out_shape=jax.ShapeDtypeStruct((slots, block,...]
    pallas_call x2, Pallas kernels: 3.95 us -> 4.46 us  [the longest x1 2.68 us: on_device(): own = blend(rounds, turn, *sources)]
  transfers between devices with their start and end apart: 4 -> 4, of which waited for: 3 -> 3; matrix products, arithmetic and copies ran while one was open for 0% -> 0% of each run, Pallas kernels for 15% -> 18%
where the time goes in v1:
time: 25.5 us; the launch traced here: 25.3 us
  waiting for transfers between devices  9.25 us (36%)
  starting transfers between devices  6.82 us (27%)
  Pallas kernels  6.65 us (26%)
  local copies, waits for them, and re-layouts  0.94 us (4%)
  other arithmetic  0.9 us (4%)
  between operations  0.71 us (3%)
    ppermute x3, starting transfers between devices, swap(): return lax.ppermute(block, axis, [(i, i ^ bit) for i in range(size)])  6.44 us
    ppermute x1, waiting for transfers between devices, on_device(): prev = lax.ppermute(own, 'blk', [(i, (i + 1) % size) for i in range(size)])  6.14 us
    ppermute x3, waiting for transfers between devices, swap(): return lax.ppermute(block, axis, [(i, i ^ bit) for i in range(size)])  3.11 us
    pallas_call x1, Pallas kernels, on_device(): own = blend(rounds, turn, *sources)  2.68 us
    pallas_call x1, Pallas kernels, on_device(): pl.pallas_call(last_kernel, out_shape=jax.ShapeDtypeStruct((slots, block,...  2.19 us
    pallas_call x1, Pallas kernels, on_device(): pl.pallas_call(first_kernel, out_shape=shapes, in_specs=[sm] * 3 + [vm] *...  1.79 us
    unnamed x8, local copies, waits for them, and re-layouts  0.93 us
    another operation x1, other arithmetic, on_device(): jnp.stack([a.reshape(block, width) for a in (prefix_key_cache, prefix_val...  0.84 us
  transfers between devices with their start and end apart: 4, of which 3 were waited for; matrix products, arithmetic and copies ran while one was open for 0% of the time, Pallas kernels for 18%

profile of v1, /device:TPU:0, one launch (start us, length us, event | category | flops | bytes accessed | tf_op | source)
XLA Modules:
  0.0 25.3 jit_solution(8411518337868023766)
XLA Ops:
  0.0 0.0 copy-start.2
  0.0 0.0 copy-start.3
  0.0 0.0 copy-start
  0.0 0.8 %pad_maximum_fusion.2 = bf16[4,32,256]{2,1,0:T(8,128)(2,1)S(1)} fusion(bf16[1,32,256]{2,1,0:T(8,128)(2,1)} %param.24, bf16[1,32,256]{2,1,0:T(8,128)(2,1)} %param.23, bf16[1,32,256]{2,1,0:T(8,128)(2,1)} %bitcast.19, bf16[1,32,256]{2,1,0:T(8,128)(2,1)} %bitcast.20), kind=kLoop, calls=%fused_computation.2 | loop fusion | flops 98304 | bytes 131072 | tf_op jit(solution)/shard_map/stack | solution.py:214
  0.9 4.1 %collective-permute-start = (bf16[2,2,32,256]{3,2,1,0:T(8,128)(2,1)S(1)}, bf16[2,2,32,256]{3,2,1,0:T(8,128)(2,1)S(1)}, u32[]{:S(2)}, u32[]{:S(2)}) collective-permute-start(bf16[2,2,32,256]{3,2,1,0:T(8,128)(2,1)S(1)} %bitcast.17), channel_id=1, source_target_pairs={{0,8},{2,10},{4,12},{6,14},{8,0},{10,2},{12,4},{14,6},{1,9},{3,11}... | collective-permute-start | bytes 196616 | tf_op jit(solution)/shard_map/ppermute | solution.py:184
  5.6 3.0 %collective-permute-done = bf16[2,2,32,256]{3,2,1,0:T(8,128)(2,1)S(1)} collective-permute-done((bf16[2,2,32,256]{3,2,1,0:T(8,128)(2,1)S(1)}, bf16[2,2,32,256]{3,2,1,0:T(8,128)(2,1)S(1)}, u32[]{:S(2)}, u32[]{:S(2)}) %collective-permute-start) | collective-permute-done | bytes 65568 | tf_op jit(solution)/shard_map/ppermute | solution.py:184
  8.7 1.8 %collective-permute-start.1 = (bf16[3,2,32,256]{3,2,1,0:T(8,128)(2,1)S(1)}, bf16[3,2,32,256]{3,2,1,0:T(8,128)(2,1)S(1)}, u32[]{:S(2)}, u32[]{:S(2)}) collective-permute-start(bf16[3,2,32,256]{3,2,1,0:T(8,128)(2,1)S(1)} %pad_maximum_fusion.1), channel_id=1, source_target_pairs={{0,2},{2,0},{4,6},{6,4},{8,10},{10,8},{12,14},{14,12},{1,3},{3,1},... | collective-permute-start | bytes 294920 | tf_op jit(solution)/shard_map/ppermute | solution.py:184
  10.4 2.7 %blend.1.own = bf16[6,2,32,256]{3,2,1,0:T(8,128)(2,1)} custom-call(s32[6]{0:T(128)} %bitcast.15, s32[1]{0:T(128)} %bitcast.7.turn, s32[6,1,32]{2,1,0:T(1,128)} %order.1, s32[6,1,32]{2,1,0:T(1,128)} %choice_at.1, bf16[64,256]{1,0:T(8,128)(2,1)} %table_k_at.1, bf16[64,256]{1,0:T(8,128)(2,1)} %table_v_at.1, bf16[6,1,32,256]{3,2,1,0:T(8,128)(2,1)} %open_k_at.1, ...), custom_call_target="tpu_custom_call" | custom-call | tf_op jit(solution)/shard_map/blend/pallas_call | solution.py:237
  13.1 0.4 %collective-permute-start.3 = (bf16[6,2,32,256]{3,2,1,0:T(8,128)(2,1)}, bf16[6,2,32,256]{3,2,1,0:T(8,128)(2,1)S(1)}, u32[]{:S(2)}, u32[]{:S(2)}) collective-permute-start(bf16[6,2,32,256]{3,2,1,0:T(8,128)(2,1)} %blend.1.own), channel_id=1, source_target_pairs={{0,2},{2,4},{4,6},{6,8},{8,10},{10,12},{12,14},{14,0},{1,3},{3,5},... | collective-permute-start | bytes 589832 | tf_op jit(solution)/shard_map/ppermute | solution.py:238
  13.5 0.1 collective-permute-done.1
  13.7 0.5 %collective-permute-start.2 = (bf16[5,2,32,256]{3,2,1,0:T(8,128)(2,1)S(1)}, bf16[5,2,32,256]{3,2,1,0:T(8,128)(2,1)S(1)}, u32[]{:S(2)}, u32[]{:S(2)}) collective-permute-start(bf16[5,2,32,256]{3,2,1,0:T(8,128)(2,1)S(1)} %pad_maximum_fusion.near), channel_id=1, source_target_pairs={{0,4},{2,6},{4,0},{6,2},{8,12},{10,14},{12,8},{14,10},{1,5},{3,7},... | collective-permute-start | bytes 491528 | tf_op jit(solution)/shard_map/ppermute | solution.py:184
  14.2 0.0 copy-done.2
  14.2 0.0 copy-done.3
  14.2 0.0 copy-done
  14.2 0.0 copy-start.1
  14.2 0.9 %copy-done.1 = bf16[6,2,32,256]{3,2,1,0:T(8,128)(2,1)S(1)} copy-done((bf16[6,2,32,256]{3,2,1,0:T(8,128)(2,1)S(1)}, bf16[6,2,32,256]{3,2,1,0:T(8,128)(2,1)}, u32[]{:S(2)}) %copy-start.1) | copy-done | bytes 196632
  15.2 1.8 %early.1 = (f32[6,2,1,224]{3,2,1,0:T(1,128)S(1)}, f32[6,2,1,224]{3,2,1,0:T(1,128)S(1)}, f32[6,2,128,224]{3,2,1,0:T(8,128)S(1)}, f32[6,1,224]{2,1,0:T(1,128)S(1)}, s32[8,128]{1,0:T(8,128)S(1)}) custom-call(s32[6]{0:T(128)S(1)} %bitcast.16, s32[1]{0:T(128)} %bitcast.7.turn, s32[1]{0:T(128)} %bitcast.9.took, s32[6,1,32]{2,1,0:T(1,128)S(1)} %copy-done.2, ...), custom_call_target="tpu_custom_call" | custom-call | tf_op jit(solution)/shard_map/early/pallas_call | solution.py:256
  16.9 6.1 %collective-permute-done.3.prev = bf16[6,2,32,256]{3,2,1,0:T(8,128)(2,1)S(1)} collective-permute-done((bf16[6,2,32,256]{3,2,1,0:T(8,128)(2,1)}, bf16[6,2,32,256]{3,2,1,0:T(8,128)(2,1)S(1)}, u32[]{:S(2)}, u32[]{:S(2)}) %collective-permute-start.3) | collective-permute-done | bytes 196640 | tf_op jit(solution)/shard_map/ppermute | solution.py:238
  23.1 0.0 collective-permute-done.2.far
  23.1 2.2 %late.1 = bf16[6,32,1792]{2,1,0:T(8,128)(2,1)} custom-call(bf16[6,32,1792]{2,1,0:T(8,128)(2,1)S(1)} %bitcast.14, bf16[5,2,32,256]{3,2,1,0:T(8,128)(2,1)S(1)} %pad_maximum_fusion.near, bf16[5,2,32,256]{3,2,1,0:T(8,128)(2,1)S(1)} %collective-permute-done.2.far, bf16[6,2,32,256]{3,2,1,0:T(8,128)(2,1)S(1)} %collective-permute-done.3.prev, ...), custom_call_target="tpu_custom_call" | custom-call | tf_op jit(solution)/shard_map/late/pallas_call | solution.py:264
  (6 shorter events, 0.1 us)
Async XLA Ops:
  0.0 14.2 %copy-start.2 = (s32[6,1,32]{2,1,0:T(1,128)S(1)}, s32[6,1,32]{2,1,0:T(1,128)}, u32[]{:S(2)}) copy-start(s32[6,1,32]{2,1,0:T(1,128)} %order.1) | copy-start | bytes 2308
  0.0 14.2 %copy-start.3 = (s32[6,1]{0,1:T(1,128)S(1)}, s32[6,1]{0,1:T(1,128)}, u32[]{:S(2)}) copy-start(s32[6,1]{0,1:T(1,128)} %param.17) | copy-start | bytes 76
  0.0 14.2 %copy-start = (bf16[6,1,32,1792]{3,2,1,0:T(8,128)(2,1)S(1)}, bf16[6,1,32,1792]{3,2,1,0:T(8,128)(2,1)}, u32[]{:S(2)}) copy-start(bf16[6,1,32,1792]{3,2,1,0:T(8,128)(2,1)} %param.13) | copy-start | bytes 2064388
  0.9 7.8 %collective-permute-start = (bf16[2,2,32,256]{3,2,1,0:T(8,128)(2,1)S(1)}, bf16[2,2,32,256]{3,2,1,0:T(8,128)(2,1)S(1)}, u32[]{:S(2)}, u32[]{:S(2)}) collective-permute-start(bf16[2,2,32,256]{3,2,1,0:T(8,128)(2,1)S(1)} %bitcast.17), channel_id=1, source_target_pairs={{0,8},{2,10},{4,12},{6,14},{8,0},{10,2},{12,4},{14,6},{1,9},{3,11}... | collective-permute-start | bytes 196616 | tf_op jit(solution)/shard_map/ppermute | solution.py:184
  8.7 5.0 %collective-permute-start.1 = (bf16[3,2,32,256]{3,2,1,0:T(8,128)(2,1)S(1)}, bf16[3,2,32,256]{3,2,1,0:T(8,128)(2,1)S(1)}, u32[]{:S(2)}, u32[]{:S(2)}) collective-permute-start(bf16[3,2,32,256]{3,2,1,0:T(8,128)(2,1)S(1)} %pad_maximum_fusion.1), channel_id=1, source_target_pairs={{0,2},{2,0},{4,6},{6,4},{8,10},{10,8},{12,14},{14,12},{1,3},{3,1},... | collective-permute-start | bytes 294920 | tf_op jit(solution)/shard_map/ppermute | solution.py:184
  13.1 10.0 %collective-permute-start.3 = (bf16[6,2,32,256]{3,2,1,0:T(8,128)(2,1)}, bf16[6,2,32,256]{3,2,1,0:T(8,128)(2,1)S(1)}, u32[]{:S(2)}, u32[]{:S(2)}) collective-permute-start(bf16[6,2,32,256]{3,2,1,0:T(8,128)(2,1)} %blend.1.own), channel_id=1, source_target_pairs={{0,2},{2,4},{4,6},{6,8},{8,10},{10,12},{12,14},{14,0},{1,3},{3,5},... | collective-permute-start | bytes 589832 | tf_op jit(solution)/shard_map/ppermute | solution.py:238
  13.7 9.4 %collective-permute-start.2 = (bf16[5,2,32,256]{3,2,1,0:T(8,128)(2,1)S(1)}, bf16[5,2,32,256]{3,2,1,0:T(8,128)(2,1)S(1)}, u32[]{:S(2)}, u32[]{:S(2)}) collective-permute-start(bf16[5,2,32,256]{3,2,1,0:T(8,128)(2,1)S(1)} %pad_maximum_fusion.near), channel_id=1, source_target_pairs={{0,4},{2,6},{4,0},{6,2},{8,12},{10,14},{12,8},{14,10},{1,5},{3,7},... | collective-permute-start | bytes 491528 | tf_op jit(solution)/shard_map/ppermute | solution.py:184
  14.2 0.9 %copy-start.1 = (bf16[6,2,32,256]{3,2,1,0:T(8,128)(2,1)S(1)}, bf16[6,2,32,256]{3,2,1,0:T(8,128)(2,1)}, u32[]{:S(2)}) copy-start(bf16[6,2,32,256]{3,2,1,0:T(8,128)(2,1)} %blend.1.own) | copy-start | bytes 589828

commit v2 on v1

--- a/solution.py
+++ b/solution.py
@@ -18,6 +18,10 @@
 SMALL = 8
 
 
+def turn_of():
+    return (lax.axis_index("blk") == lax.axis_size("blk") - 1).astype(jnp.int32)
+
+
 def column(row):
     n = row.shape[1]
     here = lax.broadcasted_iota(jnp.int32, (n, n), 0)
@@ -25,24 +29,27 @@
     return jnp.sum(jnp.where(here == there, row, 0), axis=1, keepdims=True)
 
 
-def blend_kernel(
-    rounds, turn, order_at, choice_at, table_k_at, table_v_at, open_k_at, open_v_at, own, *scratch
-):
-    sources = (order_at, choice_at, table_k_at, table_v_at, open_k_at, open_v_at)
-    order, choice, table_k, table_v, open_k, open_v, sems = scratch
+def blend_kernel(*refs):
+    count = (len(refs) - 3) // 2
+    sources, (own, keep), places = refs[:count], refs[count : count + 2], refs[count + 2 : -1]
+    sems = refs[-1]
     copies = [
         pltpu.make_async_copy(src, dst, sems.at[i])
-        for i, (src, dst) in enumerate(zip(sources, scratch))
+        for i, (src, dst) in enumerate(zip(sources, places))
     ]
     for copy in copies:
         copy.start()
     for copy in copies:
         copy.wait()
+    rounds, order, choice, table_k, table_v, open_k, open_v = places
     slots, block = open_k.shape[0], open_k.shape[2]
     nrows = table_k.shape[0]
+    turn = turn_of()
     masks, hots = [], []
     for s in range(slots):
-        masks.append(column(jnp.where(order[s] >= UNMASK * rounds[s], 1, 0)) > 0)
+        mask = jnp.where(order[s] >= UNMASK * rounds[:, s : s + 1], 1, 0)
+        keep[s] = jnp.concatenate([mask.astype(jnp.float32)] * GROUP, axis=1)
+        masks.append(column(mask) > 0)
         picked = column(choice[s])
         hots.append(
             jnp.where(picked == lax.broadcasted_iota(jnp.int32, (block, nrows), 1), 1.0, 0.0)
@@ -54,7 +61,7 @@
             mixed = jnp.where(
                 masks[s], noise[s * block : (s + 1) * block], opened[s, 0].astype(jnp.float32)
             )
-            own[lax.rem(s + turn[0], slots), i] = mixed.astype(jnp.bfloat16)
+            own[lax.rem(s + turn, slots), i] = mixed.astype(jnp.bfloat16)
 
 
 def scores(query, slot, head, keys):
@@ -102,20 +109,17 @@
     return slice(head * FEATURE_DIM, (head + 1) * FEATURE_DIM)
 
 
-def first_kernel(rounds, turn, took, order, query, near, own, tops, totals, sums, keep, mine):
+def first_kernel(took, query, near, own, tops, totals, sums, mine):
     slots, _, _, width = own.shape
     last = near.shape[0] - 1
     mine[...] = jnp.full(mine.shape, took[0], jnp.int32)
 
     def stack(s, h, i):
-        at = lax.rem(s + turn[0], slots)
+        at = lax.rem(s + turn_of(), slots)
         parts = [near[b, i, :, columns(h)] for b in range(last)] + [own[at, i, :, columns(h)]]
         return jnp.concatenate(parts, axis=0)
 
     def score(s, h):
-        if h == 0:
-            masked = jnp.where(order[s] >= UNMASK * rounds[s], 1.0, 0.0)
-            keep[s] = jnp.concatenate([masked] * GROUP, axis=1)
         return (scores(query, s, h, stack(s, h, 0)),)
 
     def peak(s, h, score):
@@ -134,7 +138,7 @@
     staggered(slots, width // FEATURE_DIM, last, (score, peak, weigh, gather))
 
 
-def last_kernel(query, near, far, prev, tops, totals, sums, keep, mine, out, made, sems):
+def last_kernel(query, near, far, prev, keep, tops, totals, sums, mine, out, made, sems):
     slots, _, block, width = prev.shape
     heads = width // FEATURE_DIM
     last = near.shape[0] - 1
@@ -205,8 +209,7 @@
     size = lax.axis_size("blk")
     me = lax.axis_index("blk")
     owner = committing_index[0]
-    rounds = rounds_finished.reshape(slots)
-    turn = (me == size - 1).astype(jnp.int32).reshape(1)
+    rounds = rounds_finished.reshape(1, slots)
 
     vm = pl.BlockSpec(memory_space=pltpu.VMEM)
     sm = pl.BlockSpec(memory_space=pltpu.SMEM)
@@ -217,7 +220,9 @@
             for a in (prefix_key_cache, prefix_value_cache, completed_keys, completed_values)
         ]
     ).reshape(2, 2, block, width)
+
     sources = (
+        rounds,
         uncover_ordering,
         random_entry_choice,
         noise_token_keys,
@@ -225,16 +230,19 @@
         unsettled_lookups,
         unsettled_payloads,
     )
-    blend = pl.pallas_call(
+    own, keep = pl.pallas_call(
         blend_kernel,
-        out_shape=jax.ShapeDtypeStruct((slots, 2, block, width), jnp.bfloat16),
-        in_specs=[sm] * 2 + [pl.BlockSpec(memory_space=pltpu.HBM)] * len(sources),
-        out_specs=vm,
+        out_shape=[
+            pltpu.VMEM((slots, 2, block, width), jnp.bfloat16),
+            pltpu.VMEM((slots, 1, GROUP * block), jnp.float32),
+        ],
+        in_specs=[pl.BlockSpec(memory_space=pltpu.HBM)] * len(sources),
+        out_specs=[vm] * 2,
         scratch_shapes=[pltpu.VMEM(a.shape, a.dtype) for a in sources]
         + [pltpu.SemaphoreType.DMA((len(sources),))],
+        compiler_params=pltpu.CompilerParams(vmem_limit_bytes=4 << 20),
         name="blend",
-    )
-    own = blend(rounds, turn, *sources)
+    )(*(pltpu.with_memory_space_constraint(a, pltpu.HBM) for a in sources))
     prev = lax.ppermute(own, "blk", [(i, (i + 1) % size) for i in range(size)])
     bits = [1 << b for b in reversed(range(size.bit_length() - 1))]
     bits[-2:] = bits[:-3:-1]
@@ -251,20 +259,19 @@
     query = probe_vectors.reshape(slots, block, wide)
     shapes = [(slots, heads, n, GROUP * block) for n in (1, 1, FEATURE_DIM)]
     shapes = [jax.ShapeDtypeStruct(a, jnp.float32) for a in shapes]
-    shapes.append(jax.ShapeDtypeStruct((slots, 1, GROUP * block), jnp.float32))
     shapes.append(jax.ShapeDtypeStruct((8, FEATURE_DIM), jnp.int32))
     state = pl.pallas_call(
         first_kernel,
         out_shape=shapes,
-        in_specs=[sm] * 3 + [vm] * 4,
+        in_specs=[sm] + [vm] * 3,
         out_specs=[vm] * len(shapes),
         compiler_params=grant(size // 2),
         name="early",
-    )(rounds, turn, took, uncover_ordering, query, packed, own)
+    )(took, query, packed, own)
     out = pl.pallas_call(
         last_kernel,
         out_shape=jax.ShapeDtypeStruct((slots, block, wide), jnp.bfloat16),
-        in_specs=[vm] * (4 + len(shapes)),
+        in_specs=[vm] * (5 + len(shapes)),
         out_specs=pl.BlockSpec(memory_space=pl.ANY),
         scratch_shapes=[
             pltpu.VMEM((slots, block, wide), jnp.bfloat16),
@@ -272,7 +279,7 @@
         ],
         compiler_params=grant(size // 2),
         name="late",
-    )(query, packed, got, prev, *state)
+    )(query, packed, got, prev, keep, *state)
     return out.reshape(slots, 1, block, wide)
 
 

time: 25.5 us -> 24.5 us (0.961)
  Pallas kernels: 6.65 us -> 5.14 us
  waiting for transfers between devices: 9.25 us -> 10.6 us
  local copies, waits for them, and re-layouts: 0.94 us -> 0.01 us
    pallas_call x2, Pallas kernels: 4.46 us -> 2.93 us  [the longest x1 1.68 us: on_device(): pl.pallas_call(blend_kernel, out_shape=[pltpu.VMEM((slots, 2, block, widt...]
    unnamed x8 -> x2, local copies, waits for them, and re-layouts: 0.93 us -> 0.01 us
    ppermute x3, waiting for transfers between devices: 3.11 us -> 3.84 us  [swap(): return lax.ppermute(block, axis, [(i, i ^ bit) for i in range(size)])]
    ppermute x1, waiting for transfers between devices: 6.14 us -> 6.77 us  [on_device(): prev = lax.ppermute(own, 'blk', [(i, (i + 1) % size) for i in range(size)])]
  transfers between devices with their start and end apart: 4 -> 4, of which waited for: 3 -> 3; matrix products, arithmetic and copies ran while one was open for 0% -> 0% of each run, Pallas kernels for 18% -> 12%
where the time goes in v2:
time: 24.5 us; the launch traced here: 24.3 us
  waiting for transfers between devices  10.6 us (43%)
  starting transfers between devices  6.91 us (28%)
  Pallas kernels  5.14 us (21%)
  other arithmetic  0.9 us (4%)
  between operations  0.7 us (3%)
    ppermute x1, waiting for transfers between devices, on_device(): prev = lax.ppermute(own, 'blk', [(i, (i + 1) % size) for i in range(size)])  6.77 us
    ppermute x3, starting transfers between devices, swap(): return lax.ppermute(block, axis, [(i, i ^ bit) for i in range(size)])  6.53 us
    ppermute x3, waiting for transfers between devices, swap(): return lax.ppermute(block, axis, [(i, i ^ bit) for i in range(size)])  3.84 us
    pallas_call x1, Pallas kernels, on_device(): pl.pallas_call(last_kernel, out_shape=jax.ShapeDtypeStruct((slots, block,...  2.21 us
    pallas_call x1, Pallas kernels, on_device(): pl.pallas_call(blend_kernel, out_shape=[pltpu.VMEM((slots, 2, block, widt...  1.68 us
    pallas_call x1, Pallas kernels, on_device(): pl.pallas_call(first_kernel, out_shape=shapes, in_specs=[sm] + [vm] * 3,...  1.26 us
    another operation x1, other arithmetic, on_device(): jnp.stack([a.reshape(block, width) for a in (prefix_key_cache, prefix_val...  0.84 us
  transfers between devices with their start and end apart: 4, of which 3 were waited for; matrix products, arithmetic and copies ran while one was open for 0% of the time, Pallas kernels for 12%

profile of v2, /device:TPU:0, one launch (start us, length us, event | category | flops | bytes accessed | tf_op | source)
XLA Modules:
  0.0 24.3 jit_solution(6264991428293303875)
XLA Ops:
  0.0 0.0 copy-start
  0.0 0.8 %pad_maximum_fusion.2 = bf16[4,32,256]{2,1,0:T(8,128)(2,1)S(1)} fusion(bf16[1,32,256]{2,1,0:T(8,128)(2,1)} %param.24, bf16[1,32,256]{2,1,0:T(8,128)(2,1)} %param.23, bf16[1,32,256]{2,1,0:T(8,128)(2,1)} %bitcast.16, bf16[1,32,256]{2,1,0:T(8,128)(2,1)} %bitcast.17), kind=kLoop, calls=%fused_computation.2 | loop fusion | flops 98304 | bytes 131072 | tf_op jit(solution)/shard_map/stack | solution.py:217
  0.8 4.1 %collective-permute-start = (bf16[2,2,32,256]{3,2,1,0:T(8,128)(2,1)S(1)}, bf16[2,2,32,256]{3,2,1,0:T(8,128)(2,1)S(1)}, u32[]{:S(2)}, u32[]{:S(2)}) collective-permute-start(bf16[2,2,32,256]{3,2,1,0:T(8,128)(2,1)S(1)} %bitcast.14), channel_id=1, source_target_pairs={{0,8},{2,10},{4,12},{6,14},{8,0},{10,2},{12,4},{14,6},{1,9},{3,11}... | collective-permute-start | bytes 196616 | tf_op jit(solution)/shard_map/ppermute | solution.py:188
  5.6 3.0 %collective-permute-done = bf16[2,2,32,256]{3,2,1,0:T(8,128)(2,1)S(1)} collective-permute-done((bf16[2,2,32,256]{3,2,1,0:T(8,128)(2,1)S(1)}, bf16[2,2,32,256]{3,2,1,0:T(8,128)(2,1)S(1)}, u32[]{:S(2)}, u32[]{:S(2)}) %collective-permute-start) | collective-permute-done | bytes 65568 | tf_op jit(solution)/shard_map/ppermute | solution.py:188
  8.7 1.8 %collective-permute-start.1 = (bf16[3,2,32,256]{3,2,1,0:T(8,128)(2,1)S(1)}, bf16[3,2,32,256]{3,2,1,0:T(8,128)(2,1)S(1)}, u32[]{:S(2)}, u32[]{:S(2)}) collective-permute-start(bf16[3,2,32,256]{3,2,1,0:T(8,128)(2,1)S(1)} %pad_maximum_fusion.1), channel_id=1, source_target_pairs={{0,2},{2,0},{4,6},{6,4},{8,10},{10,8},{12,14},{14,12},{1,3},{3,1},... | collective-permute-start | bytes 294920 | tf_op jit(solution)/shard_map/ppermute | solution.py:188
  10.4 1.7 %blend.1 = (bf16[6,2,32,256]{3,2,1,0:T(8,128)(2,1)S(1)}, f32[6,1,224]{2,1,0:T(1,128)S(1)}) custom-call(s32[1,6]{1,0:T(1,128)} %bitcast.18, s32[6,1,32]{2,1,0:T(1,128)} %refs_1_.1, s32[6,1,32]{2,1,0:T(1,128)} %refs_2_.1, bf16[64,256]{1,0:T(8,128)(2,1)} %refs_3_.1, bf16[64,256]{1,0:T(8,128)(2,1)} %refs_4_.1, bf16[6,1,32,256]{3,2,1,0:T(8,128)(2,1)} %refs_5_.1, ...), custom_call_target="tpu_custom_call" | custom-call | tf_op jit(solution)/shard_map/blend/pallas_call | solution.py:233
  12.1 0.4 %collective-permute-start.3 = (bf16[6,2,32,256]{3,2,1,0:T(8,128)(2,1)S(1)}, bf16[6,2,32,256]{3,2,1,0:T(8,128)(2,1)S(1)}, u32[]{:S(2)}, u32[]{:S(2)}) collective-permute-start(bf16[6,2,32,256]{3,2,1,0:T(8,128)(2,1)S(1)} %get-tuple-element.11.own), channel_id=1, source_target_pairs={{0,2},{2,4},{4,6},{6,8},{8,10},{10,12},{12,14},{14,0},{1,3},{3,5},... | collective-permute-start | bytes 589832 | tf_op jit(solution)/shard_map/ppermute | solution.py:246
  12.5 0.8 %collective-permute-done.1 = bf16[3,2,32,256]{3,2,1,0:T(8,128)(2,1)S(1)} collective-permute-done((bf16[3,2,32,256]{3,2,1,0:T(8,128)(2,1)S(1)}, bf16[3,2,32,256]{3,2,1,0:T(8,128)(2,1)S(1)}, u32[]{:S(2)}, u32[]{:S(2)}) %collective-permute-start.1) | collective-permute-done | bytes 98336 | tf_op jit(solution)/shard_map/ppermute | solution.py:188
  13.4 0.6 %collective-permute-start.2 = (bf16[5,2,32,256]{3,2,1,0:T(8,128)(2,1)S(1)}, bf16[5,2,32,256]{3,2,1,0:T(8,128)(2,1)S(1)}, u32[]{:S(2)}, u32[]{:S(2)}) collective-permute-start(bf16[5,2,32,256]{3,2,1,0:T(8,128)(2,1)S(1)} %pad_maximum_fusion.near), channel_id=1, source_target_pairs={{0,4},{2,6},{4,0},{6,2},{8,12},{10,14},{12,8},{14,10},{1,5},{3,7},... | collective-permute-start | bytes 491528 | tf_op jit(solution)/shard_map/ppermute | solution.py:188
  14.0 0.0 copy-done
  14.0 1.3 %early.1 = (f32[6,2,1,224]{3,2,1,0:T(1,128)S(1)}, f32[6,2,1,224]{3,2,1,0:T(1,128)S(1)}, f32[6,2,128,224]{3,2,1,0:T(8,128)S(1)}, s32[8,128]{1,0:T(8,128)S(1)}) custom-call(s32[1]{0:T(128)} %bitcast.8.took, bf16[6,32,1792]{2,1,0:T(8,128)(2,1)S(1)} %bitcast.12, bf16[5,2,32,256]{3,2,1,0:T(8,128)(2,1)S(1)} %pad_maximum_fusion.near, ...), custom_call_target="tpu_custom_call" | custom-call | tf_op jit(solution)/shard_map/early/pallas_call | solution.py:263
  15.3 6.8 %collective-permute-done.3.prev = bf16[6,2,32,256]{3,2,1,0:T(8,128)(2,1)S(1)} collective-permute-done((bf16[6,2,32,256]{3,2,1,0:T(8,128)(2,1)S(1)}, bf16[6,2,32,256]{3,2,1,0:T(8,128)(2,1)S(1)}, u32[]{:S(2)}, u32[]{:S(2)}) %collective-permute-start.3) | collective-permute-done | bytes 196640 | tf_op jit(solution)/shard_map/ppermute | solution.py:246
  22.1 0.0 collective-permute-done.2.far
  22.1 2.2 %late.1 = bf16[6,32,1792]{2,1,0:T(8,128)(2,1)} custom-call(bf16[6,32,1792]{2,1,0:T(8,128)(2,1)S(1)} %bitcast.13, bf16[5,2,32,256]{3,2,1,0:T(8,128)(2,1)S(1)} %pad_maximum_fusion.near, bf16[5,2,32,256]{3,2,1,0:T(8,128)(2,1)S(1)} %collective-permute-done.2.far, bf16[6,2,32,256]{3,2,1,0:T(8,128)(2,1)S(1)} %collective-permute-done.3.prev, ...), custom_call_target="tpu_custom_call" | custom-call | tf_op jit(solution)/shard_map/late/pallas_call | solution.py:271
  (6 shorter events, 0.1 us)
Async XLA Ops:
  0.0 14.0 %copy-start = (bf16[6,1,32,1792]{3,2,1,0:T(8,128)(2,1)S(1)}, bf16[6,1,32,1792]{3,2,1,0:T(8,128)(2,1)}, u32[]{:S(2)}) copy-start(bf16[6,1,32,1792]{3,2,1,0:T(8,128)(2,1)} %param.13) | copy-start | bytes 2064388
  0.8 7.8 %collective-permute-start = (bf16[2,2,32,256]{3,2,1,0:T(8,128)(2,1)S(1)}, bf16[2,2,32,256]{3,2,1,0:T(8,128)(2,1)S(1)}, u32[]{:S(2)}, u32[]{:S(2)}) collective-permute-start(bf16[2,2,32,256]{3,2,1,0:T(8,128)(2,1)S(1)} %bitcast.14), channel_id=1, source_target_pairs={{0,8},{2,10},{4,12},{6,14},{8,0},{10,2},{12,4},{14,6},{1,9},{3,11}... | collective-permute-start | bytes 196616 | tf_op jit(solution)/shard_map/ppermute | solution.py:188
  8.7 4.7 %collective-permute-start.1 = (bf16[3,2,32,256]{3,2,1,0:T(8,128)(2,1)S(1)}, bf16[3,2,32,256]{3,2,1,0:T(8,128)(2,1)S(1)}, u32[]{:S(2)}, u32[]{:S(2)}) collective-permute-start(bf16[3,2,32,256]{3,2,1,0:T(8,128)(2,1)S(1)} %pad_maximum_fusion.1), channel_id=1, source_target_pairs={{0,2},{2,0},{4,6},{6,4},{8,10},{10,8},{12,14},{14,12},{1,3},{3,1},... | collective-permute-start | bytes 294920 | tf_op jit(solution)/shard_map/ppermute | solution.py:188
  12.1 10.0 %collective-permute-start.3 = (bf16[6,2,32,256]{3,2,1,0:T(8,128)(2,1)S(1)}, bf16[6,2,32,256]{3,2,1,0:T(8,128)(2,1)S(1)}, u32[]{:S(2)}, u32[]{:S(2)}) collective-permute-start(bf16[6,2,32,256]{3,2,1,0:T(8,128)(2,1)S(1)} %get-tuple-element.11.own), channel_id=1, source_target_pairs={{0,2},{2,4},{4,6},{6,8},{8,10},{10,12},{12,14},{14,0},{1,3},{3,5},... | collective-permute-start | bytes 589832 | tf_op jit(solution)/shard_map/ppermute | solution.py:246
  13.4 8.7 %collective-permute-start.2 = (bf16[5,2,32,256]{3,2,1,0:T(8,128)(2,1)S(1)}, bf16[5,2,32,256]{3,2,1,0:T(8,128)(2,1)S(1)}, u32[]{:S(2)}, u32[]{:S(2)}) collective-permute-start(bf16[5,2,32,256]{3,2,1,0:T(8,128)(2,1)S(1)} %pad_maximum_fusion.near), channel_id=1, source_target_pairs={{0,4},{2,6},{4,0},{6,2},{8,12},{10,14},{12,8},{14,10},{1,5},{3,7},... | collective-permute-start | bytes 491528 | tf_op jit(solution)/shard_map/ppermute | solution.py:188
